TPU v7x, 256 devices: a whole 4x4x8 slice. The times are simulated.
256 devices in a mesh: leaf: 4 (over x), front: 64 (over z, y, core).
Axes of the slice: x: 4, y: 4, z: 8, core: 2. Of those that a mesh axis runs over, the one named last changes fastest.
Arguments:
- front: float32 [16384, 16384], P('leaf', 'front'), as said below
- updates: float32 [8192, 128, 128], P(('leaf', 'front')), may hold values from -4 to 4
- target_owner: int32 [8192], P(('leaf', 'front')), may hold values from 0 to 63, as said below
- target_slot: int32 [8192], P(('leaf', 'front')), may hold values from 0 to 63
Outputs:
- factored: float32 [16384, 16384], P('leaf', 'front')
Inputs may be any that keep to these rules, and one draw needn't show every extreme that they name: `target_owner`: among the 32 blocks of one device every owner index appears at most once; in every group of devices sharing an index of leaf, some owner index is named by every device of the group. The front is symmetric.
All inputs are finite; a program needn't handle non-finite values.
Results may differ from a plain program's by a relative error of at most 0.00015.
Values sent between devices are 32-bit elements; how exact they have to be, the bound alone decides.
A program may use at most 128 MiB of HBM per device.

v0:
```python
import jax
import jax.numpy as jnp
from jax import lax
from jax.sharding import PartitionSpec as P


def spread(value, axis, source):
    kept = jnp.where(lax.axis_index(axis) == source, value, 0).astype(value.dtype)
    return lax.psum(kept, axis)


def assemble(front, updates, target_owner, target_slot):
    nrows, width = front.shape
    tile = updates.shape[1]
    nfront = lax.axis_size("front")
    buffer = jnp.zeros((nfront, tile, tile), jnp.float32).at[target_owner].set(updates)
    labels = jnp.zeros((nfront,), jnp.float32).at[target_owner].set(target_slot.astype(jnp.float32))
    arrived, places = (
        lax.all_to_all(buffer, "front", split_axis=0, concat_axis=0, tiled=True),
        lax.all_to_all(labels, "front", split_axis=0, concat_axis=0, tiled=True),
    )
    places = places.astype(jnp.int32)
    col_tiles = width // tile
    grid = front.reshape(nrows // tile, tile, col_tiles, tile)
    grid = grid.at[places // col_tiles, :, places % col_tiles, :].add(arrived)
    return grid.reshape(nrows, width)


def eliminate(shard, panel, start, row_ids, col_ids, column):
    nrows, width = panel.shape
    diag = spread(panel[start : start + width], "leaf", 0)
    chol = jnp.linalg.cholesky(diag)
    eye = jnp.eye(width, dtype=jnp.float32)
    inverse = lax.linalg.triangular_solve(chol, eye, left_side=True, lower=True)
    prod = jnp.dot(panel, inverse.T, precision=lax.Precision.HIGHEST)
    lower = jnp.where(row_ids[:, None] >= start, prod, panel)
    owner_row = column * width // nrows
    offset = column * width - owner_row * nrows
    mine = lax.dynamic_slice_in_dim(lower, offset, width, 0)
    across = spread(mine, "leaf", owner_row)
    trail = jnp.where(row_ids[:, None] >= start + width, lower, 0.0)
    updated = shard - jnp.dot(trail, across.T, precision=lax.Precision.HIGHEST)
    updated = jnp.where(col_ids[None, :] >= start + width, updated, shard)
    return (jnp.where(column == start // width, lower, updated), lower)


def shards(front, updates, target_owner, target_slot):
    nrows, width = front.shape
    column = lax.axis_index("front")
    row_ids = lax.axis_index("leaf") * nrows + jnp.arange(nrows, dtype=jnp.int32)
    col_ids = column * width + jnp.arange(width, dtype=jnp.int32)
    shard = assemble(front, updates, target_owner, target_slot)
    first = spread(shard, "front", 0)
    shard, lower = eliminate(shard, first, 0, row_ids, col_ids, column)
    second = spread(shard, "front", 1)
    shard, lower = eliminate(shard, second, width, row_ids, col_ids, column)
    return shard


def solution(mesh):
    return jax.shard_map(
        shards,
        mesh=mesh,
        in_specs=(
            P("leaf", "front"),
            P(("leaf", "front"), None, None),
            P(("leaf", "front")),
            P(("leaf", "front")),
        ),
        out_specs=P("leaf", "front"),
        check_vma=False,
    )
```

profile of v0, /device:TPU:65, one launch (start us, length us, event | category | flops | bytes accessed | tf_op | source)
XLA Modules:
  0.0 928.0 jit_solution(8571510435331064767)
XLA Ops:
  9.4 11.6 %all-to-all-start = ((f32[64,1,1]{2,1,0:T(1,128)}), f32[64,1,1]{2,1,0:T(1,128)S(1)}, u32[]{:S(2)}, u32[]{:S(2)}) async-start(f32[64,1,1]{2,1,0:T(1,128)} %copy.35), calls=%async_computation | async-start | bytes 65536 | tf_op jit(solution)/shard_map/all_to_all | solution.py:20
  21.0 2.5 broadcast_in_dim.75
  23.5 5.4 scatter_fusion
  28.9 10.5 %all-to-all-start.1 = ((f32[64,128,128]{2,1,0:T(8,128)}), f32[64,128,128]{2,1,0:T(8,128)}, u32[]{:S(2)}, u32[]{:S(2)}) async-start(f32[64,128,128]{2,1,0:T(8,128)} %scatter_fusion), calls=%async_computation.1 | async-start | bytes 8388608 | tf_op jit(solution)/shard_map/all_to_all | solution.py:19
  39.4 5.8 reshape.200
  45.2 4.7 copy.36
  51.2 81.1 %all-to-all-done.1 = f32[64,128,128]{2,1,0:T(8,128)} async-done(((f32[64,128,128]{2,1,0:T(8,128)}), f32[64,128,128]{2,1,0:T(8,128)}, u32[]{:S(2)}, u32[]{:S(2)}) %all-to-all-start.1) | async-done | bytes 4194336 | tf_op jit(solution)/shard_map/all_to_all | solution.py:19
  132.3 13.8 %scatter_fusion.1 = f32[32,128,2,128]{3,1,2,0:T(8,128)} fusion(f32[32,128,2,128]{3,1,2,0:T(8,128)} %copy.36, s32[64]{0:T(128)S(1)} %fusion.37, f32[64,128,128]{2,1,0:T(8,128)} %all-to-all-done.1), kind=kCustom, calls=%fused_computation.2 | custom fusion | flops 1048576 | bytes 12583424 | tf_op jit(solution)/shard_map/scatter-add | solution.py:25
  146.0 5.4 copy.37
  151.5 8.0 bitcast_select_fusion
  159.6 195.4 %all-reduce.8.cloned.1.call-done = f32[4096,256]{0,1:T(8,128)} async-done(((f32[4096,256]{0,1:T(8,128)}), f32[4096,256]{0,1:T(8,128)}) %all-reduce.8.cloned.1.call-update) | async-done | bytes 4194320 | tf_op jit(solution)/shard_map/psum | solution.py:9
  357.3 44.1 %all-reduce.10.cloned.1.call-done = f32[256,256]{0,1:T(8,128)} async-done(((f32[256,256]{0,1:T(8,128)}), f32[256,256]{0,1:T(8,128)}) %all-reduce.10.cloned.1.call-update) | async-done | bytes 262160 | tf_op jit(solution)/shard_map/psum | solution.py:9
  403.5 11.7 %cholesky.130 = f32[128,128]{1,0:T(8,128)S(1)} custom-call(f32[128,128]{1,0:T(8,128)S(1)} %cholesky.194), custom_call_target="Cholesky" | custom-call | tf_op jit(solution)/shard_map/jit(cholesky)/cholesky | solution.py:32
  415.3 9.8 %custom-call.15 = f32[1,128,128]{1,2,0:T(8,128)S(1)} custom-call(f32[1,128,128]{2,1,0:T(8,128)S(1)} %get-tuple-element.50), custom_call_target="InvertDiagBlocksLowerTriangular" | custom-call | tf_op jit(solution)/shard_map/jit(cholesky)/cholesky | solution.py:32
  425.6 11.7 %cholesky.147 = f32[128,128]{1,0:T(8,128)S(1)} custom-call(f32[128,128]{1,0:T(8,128)S(1)} %convolution_subtract_fusion.3), custom_call_target="Cholesky" | custom-call | tf_op jit(solution)/shard_map/jit(cholesky)/cholesky | solution.py:32
  439.4 4.0 while.4
  443.5 19.7 %custom-call.16 = f32[2,128,128]{1,2,0:T(8,128)S(1)} custom-call(f32[2,128,128]{2,1,0:T(8,128)S(1)} %get-tuple-element.21), custom_call_target="InvertDiagBlocksLowerTriangular" | custom-call | tf_op jit(solution)/shard_map/triangular_solve/custom-call.0 | solution.py:34
  464.0 8.3 convolution_select_fusion.1
  475.1 47.5 %all-reduce.12.cloned.1.call-done = f32[256,256]{0,1:T(8,128)} async-done(((f32[256,256]{0,1:T(8,128)}), f32[256,256]{0,1:T(8,128)}) %all-reduce.12.cloned.1.call-update) | async-done | bytes 262160 | tf_op jit(solution)/shard_map/psum | solution.py:9
  522.6 14.6 %broadcast_select_fusion = (f32[4096,256]{0,1:T(8,128)}, f32[4096,256]{0,1:T(8,128)}) fusion(pred[]{:T(512)S(6)} %eq.24, f32[4096,256]{0,1:T(8,128)} %copy-done.1, f32[256,256]{0,1:T(8,128)} %all-reduce.12.cloned.1.call-done, pred[4096]{0:T(1024)(128)(4,1)S(1)} %fusion.33, f32[32,8,32,128]{3,2,1,0:T(8,128)} %bitcast.92, pred[256]{0:T(512)(128)(4,1)S(1)} %fusion.35, ...), kind=kOutput, calls=%fused_computation.17 | convolution fusion | flops 3226468352 | bytes 17043714 | tf_op jit(solution)/shard_map/dot_general | solution.py:42
  537.3 198.6 %all-reduce.14.cloned.1.call-done = f32[4096,256]{0,1:T(8,128)} async-done(((f32[4096,256]{0,1:T(8,128)}), f32[4096,256]{0,1:T(8,128)}) %all-reduce.14.cloned.1.call-update) | async-done | bytes 4194320 | tf_op jit(solution)/shard_map/psum | solution.py:9
  737.8 44.3 %all-reduce.16.cloned.1.call-done = f32[256,256]{0,1:T(8,128)} async-done(((f32[256,256]{0,1:T(8,128)}), f32[256,256]{0,1:T(8,128)}) %all-reduce.16.cloned.1.call-update) | async-done | bytes 262160 | tf_op jit(solution)/shard_map/psum | solution.py:9
  784.2 11.7 %cholesky.164 = f32[128,128]{1,0:T(8,128)S(1)} custom-call(f32[128,128]{1,0:T(8,128)S(1)} %cholesky.197), custom_call_target="Cholesky" | custom-call | tf_op jit(solution)/shard_map/jit(cholesky)/cholesky | solution.py:32
  796.0 9.8 %custom-call.17 = f32[1,128,128]{1,2,0:T(8,128)S(1)} custom-call(f32[1,128,128]{2,1,0:T(8,128)S(1)} %get-tuple-element.46), custom_call_target="InvertDiagBlocksLowerTriangular" | custom-call | tf_op jit(solution)/shard_map/jit(cholesky)/cholesky | solution.py:32
  806.3 11.7 %cholesky.181 = f32[128,128]{1,0:T(8,128)S(1)} custom-call(f32[128,128]{1,0:T(8,128)S(1)} %convolution_subtract_fusion.2), custom_call_target="Cholesky" | custom-call | tf_op jit(solution)/shard_map/jit(cholesky)/cholesky | solution.py:32
  820.5 4.1 while.5
  824.6 19.7 %custom-call.18 = f32[2,128,128]{1,2,0:T(8,128)S(1)} custom-call(f32[2,128,128]{2,1,0:T(8,128)S(1)} %get-tuple-element.22), custom_call_target="InvertDiagBlocksLowerTriangular" | custom-call | tf_op jit(solution)/shard_map/triangular_solve/custom-call.0 | solution.py:34
  845.2 8.4 convolution_select_fusion
  853.6 2.0 copy-done
  856.4 47.6 %all-reduce.18.cloned.1.call-done = f32[256,256]{0,1:T(8,128)} async-done(((f32[256,256]{0,1:T(8,128)}), f32[256,256]{0,1:T(8,128)}) %all-reduce.18.cloned.1.call-update) | async-done | bytes 262160 | tf_op jit(solution)/shard_map/psum | solution.py:9
  903.9 11.2 %fusion.1 = f32[4096,256]{0,1:T(8,128)} fusion(f32[4096,256]{0,1:T(8,128)} %copy-done, f32[4096,256]{0,1:T(8,128)} %get-tuple-element.54, f32[256,256]{0,1:T(8,128)} %all-reduce.18.cloned.1.call-done, pred[256]{0:T(512)(128)(4,1)S(1)} %fusion.34, pred[4096]{0:T(1024)(128)(4,1)S(1)} %fusion.31, pred[]{:T(512)S(6)} %eq.24), kind=kOutput, calls=%fused_computation.12 | convolution fusion | flops 3225419776 | bytes 12849409 | tf_op jit(solution)/shard_map/dot_general | solution.py:42
  915.1 5.6 copy.44
  (77 shorter events, 28.6 us)
Async XLA Ops:
  6.5 17.0 %copy-start.2 = (f32[32,128,128]{2,1,0:T(8,128)S(1)}, f32[32,128,128]{2,1,0:T(8,128)}, u32[]{:S(2)}) copy-start(f32[32,128,128]{2,1,0:T(8,128)} %param.8) | copy-start | bytes 6291460
  9.4 19.5 %all-to-all-start = ((f32[64,1,1]{2,1,0:T(1,128)}), f32[64,1,1]{2,1,0:T(1,128)S(1)}, u32[]{:S(2)}, u32[]{:S(2)}) async-start(f32[64,1,1]{2,1,0:T(1,128)} %copy.35), calls=%async_computation | async-start | bytes 65536 | tf_op jit(solution)/shard_map/all_to_all | solution.py:20
  28.9 103.4 %all-to-all-start.1 = ((f32[64,128,128]{2,1,0:T(8,128)}), f32[64,128,128]{2,1,0:T(8,128)}, u32[]{:S(2)}, u32[]{:S(2)}) async-start(f32[64,128,128]{2,1,0:T(8,128)} %scatter_fusion), calls=%async_computation.1 | async-start | bytes 8388608 | tf_op jit(solution)/shard_map/all_to_all | solution.py:19
  39.4 315.7 %all-reduce.8.cloned.1.call-start = ((), (), s32[]{:S(2)}) async-start(), calls=%async_computation.2 | async-start | bytes 8388608 | tf_op jit(solution)/shard_map/psum | solution.py:9
  159.6 241.9 %all-reduce.10.cloned.1.call-start = ((), (), s32[]{:S(2)}) async-start(), calls=%async_computation.3 | async-start | bytes 524288 | tf_op jit(solution)/shard_map/psum | solution.py:9
  356.7 165.9 %all-reduce.12.cloned.1.call-start = ((), (), s32[]{:S(2)}) async-start(), calls=%async_computation.4 | async-start | bytes 524288 | tf_op jit(solution)/shard_map/psum | solution.py:9
  472.4 2.0 copy-start.1
  475.1 260.8 %all-reduce.14.cloned.1.call-start = ((), (), s32[]{:S(2)}) async-start(), calls=%async_computation.5 | async-start | bytes 8388608 | tf_op jit(solution)/shard_map/psum | solution.py:9
  537.2 244.9 %all-reduce.16.cloned.1.call-start = ((), (), s32[]{:S(2)}) async-start(), calls=%async_computation.6 | async-start | bytes 524288 | tf_op jit(solution)/shard_map/psum | solution.py:9
  737.5 166.4 %all-reduce.18.cloned.1.call-start = ((), (), s32[]{:S(2)}) async-start(), calls=%async_computation.7 | async-start | bytes 524288 | tf_op jit(solution)/shard_map/psum | solution.py:9
  853.6 2.0 copy-start
Sparse Core Ops, SparseCore 0:
  159.7 195.3 all-reduce.7
  357.4 44.0 all-reduce.9
  475.2 47.4 all-reduce.11
  537.4 198.4 all-reduce.13
  738.0 44.0 all-reduce.15
  856.5 47.4 all-reduce.17
where the time goes:
time: 939 us; the launch traced here: 928 us
  waiting for transfers between devices  659 us (70%)
  other arithmetic  139 us (15%)
  matrix products  45.1 us (5%)
  local copies, waits for them, and re-layouts  44.6 us (5%)
  starting transfers between devices  23 us (2%)
  between operations  16.7 us (2%)
    psum x6, waiting for transfers between devices, spread(): return lax.psum(kept, axis)  577 us
    all_to_all x1, waiting for transfers between devices, assemble(): lax.all_to_all(buffer, 'front', split_axis=0, concat_axis=0, tiled=True)  81.1 us
    another operation x13, other arithmetic, eliminate(): chol = jnp.linalg.cholesky(diag)  68.5 us
    another operation x5, other arithmetic, eliminate(): inverse = lax.linalg.triangular_solve(chol, eye, left_side=True, lower=True)  39.4 us
    dot_general x2, matrix products, eliminate(): updated = shard - jnp.dot(trail, across.T, precision=lax.Precision.HIGHEST)  25.7 us
  transfers between devices with their start and end apart: 8, of which 7 were waited for; matrix products, arithmetic and copies ran while one was open for 2% of the time, Pallas kernels for 0%

commit v1 on v0

v1 whole, which is shorter than its diff:
```python
import functools
import jax
import jax.numpy as jnp
from jax import lax
from jax.experimental import pallas as pl
from jax.experimental.pallas import tpu as pltpu
from jax.sharding import PartitionSpec as P

HI = lax.Precision.HIGHEST
def sort_kernel(owner_ref, slot_ref, updates_ref, top_ref, big_ref, small_ref, turned_ref, place_ref, sem):
    sends = updates_ref.shape[0]
    peers = big_ref.shape[0]
    tile = 128

    def send(j, carry):
        pltpu.make_async_copy(updates_ref.at[j], big_ref.at[owner_ref[j]], sem).start()
        return carry

    lax.fori_loop(0, sends, send, 0)

    def clear(d, carry):
        place_ref[d] = -1
        return carry

    lax.fori_loop(0, peers, clear, 0)

    def mark(j, carry):
        place_ref[owner_ref[j]] = j
        return carry

    lax.fori_loop(0, sends, mark, 0)

    def label(d):
        j = place_ref[d]
        return jnp.where(j >= 0, slot_ref[jnp.maximum(j, 0)], -1).astype(jnp.float32)

    row = lax.broadcasted_iota(jnp.int32, (8, tile), 0)
    for o in range(2):
        j = place_ref[o]
        block = jnp.where(j >= 0, updates_ref[jnp.maximum(j, 0)], 0.0)
        near = label(o)
        for a in range(16):
            for h in range(2):
                d = 4 * a + 2 * o + h
                small_ref[d, 0:8, :] = block[8 * a : 8 * a + 8, :]
                small_ref[d, 8:16, :] = jnp.where(row == 0, near, label(d))
    turned_ref[...] = top_ref[...].T
    pltpu.make_async_copy(updates_ref, big_ref.at[pl.ds(0, sends)], sem).wait()


def sort_blocks(owner, slot, updates, front, peers):
    f32 = jnp.float32
    width = front.shape[1]
    sends, tile = updates.shape[:2]
    smem = pl.BlockSpec(memory_space=pltpu.SMEM)
    vm = pl.BlockSpec(memory_space=pltpu.VMEM)
    return pl.pallas_call(
        sort_kernel,
        grid=(1,),
        out_shape=(
            jax.ShapeDtypeStruct((peers, tile, tile), f32),
            jax.ShapeDtypeStruct((peers, 16, tile), f32),
            jax.ShapeDtypeStruct((width, 2 * width), f32),
        ),
        in_specs=[smem, smem, pl.BlockSpec((sends, tile, tile), lambda i: (0, 0, 0)), pl.BlockSpec((2 * width, width), lambda i: (0, 0))],
        out_specs=(
            pl.BlockSpec(memory_space=pl.ANY),
            pl.BlockSpec((peers, 16, tile), lambda i: (0, 0, 0)),
            pl.BlockSpec((width, 2 * width), lambda i: (0, 0)),
        ),
        scratch_shapes=[pltpu.SMEM((peers,), jnp.int32), pltpu.SemaphoreType.DMA],
        name="sort_blocks",
    )(owner, slot, updates, front)


def split(x):
    high = x.astype(jnp.bfloat16)
    return high, (x - high.astype(jnp.float32)).astype(jnp.bfloat16)


def product(a, b):
    ah, al = split(a)
    bh, bl = b
    f32 = jnp.float32
    return (
        jnp.dot(ah, bh, preferred_element_type=f32)
        + jnp.dot(ah, bl, preferred_element_type=f32)
        + jnp.dot(al, bh, preferred_element_type=f32)
    )


def finish_kernel(where_ref, label_ref, front_ref, panel_ref, arrived_ref, high_ref, low_ref, out_ref, total_ref):
    step = pl.program_id(0)
    tile = 128

    @pl.when(step == 0)
    def _():
        total_ref[...] = jnp.zeros_like(total_ref)

        def add(j, carry):
            slot = label_ref[j]

            @pl.when(slot >= 0)
            def _():
                total_ref[slot] += arrived_ref[j]

            return carry

        lax.fori_loop(0, arrived_ref.shape[0], add, 0)

    column, band = where_ref[0], where_ref[1]
    kind = jnp.where(band == 0, jnp.minimum(step, 2), 2)
    minus = product(panel_ref[...], (high_ref[kind], low_ref[kind]))
    keep = jnp.logical_or(column >= 2, jnp.logical_and(column == 1, kind == 0))
    for h in range(2):
        for k in range(2):
            rows = slice(h * tile, h * tile + tile)
            cols = slice(k * tile, k * tile + tile)
            base = front_ref[rows, cols] + total_ref[step * 4 + h * 2 + k]
            out_ref[rows, cols] = jnp.where(keep, base, 0.0) - minus[rows, cols]


def finish(where, labels, front, panel, arrived, high, low):
    nrows, width = front.shape
    peers, tile = arrived.shape[:2]
    smem = pl.BlockSpec(memory_space=pltpu.SMEM)
    one = pl.Buffered(buffer_count=1)
    return pl.pallas_call(
        finish_kernel,
        grid=(nrows // 256,),
        out_shape=jax.ShapeDtypeStruct((nrows, width), jnp.float32),
        in_specs=[
            smem,
            smem,
            pl.BlockSpec((256, width), lambda i: (i, 0)),
            pl.BlockSpec((256, 2 * width), lambda i: (i, 0)),
            pl.BlockSpec(arrived.shape, lambda i: (0, 0, 0), pipeline_mode=one),
            pl.BlockSpec(high.shape, lambda i: (0, 0, 0), pipeline_mode=one),
            pl.BlockSpec(low.shape, lambda i: (0, 0, 0), pipeline_mode=one),
        ],
        out_specs=pl.BlockSpec((256, width), lambda i: (i, 0)),
        scratch_shapes=[pltpu.VMEM((64, tile, tile), jnp.float32)],
        name="finish",
    )(where, labels, front, panel, arrived, high, low)


NZ, NY, NC = 8, 4, 2


def panel_kernel(leafs, small_ref, turned_ref, panel_ref, diag_ref, mine_ref, got_ref, old_ref, part_ref, sems):
    peers = got_ref.shape[0]
    tile = 128
    x = lax.axis_index("leaf")
    f = lax.axis_index("front")
    z, y, c = f // (NY * NC), (f // NC) % NY, f % NC
    a, q = f // 4, f % 4
    half = y // 2

    def lanes(index):
        return pl.ds(pl.multiple_of(index * tile, tile), tile)

    def device(z2, y2, c2):
        return (z2 * NY + y2) * NC + c2

    def remote(src, dst, stage, target):
        pltpu.make_async_remote_copy(
            src_ref=src, dst_ref=dst, send_sem=sems.at[0, stage], recv_sem=sems.at[1, stage],
            device_id=target, device_id_type=pl.DeviceIdType.MESH,
        ).start()

    def local(src, dst, stage):
        pltpu.make_async_copy(src, dst, sems.at[1, stage]).start()

    def wait(ref, which, stage):
        pltpu.make_async_copy(ref, ref, sems.at[which, stage]).wait()

    local(small_ref.at[f], got_ref.at[f], 0)

    def send_slices(k, carry):
        d = lax.rem(f + k, peers)
        remote(small_ref.at[d], got_ref.at[f], 0, (x, d))
        return carry

    lax.fori_loop(1, peers, send_slices, 0)

    band, place = f // 16, f % 16

    @pl.when(x == 0)
    def _():
        def send_old(k, carry):
            i = lax.rem(f + k, peers)
            src = turned_ref.at[:, i // 4, :, lanes(i % 4)]
            dst = old_ref.at[pl.ds(2 * place, 2)]
            self_ = jnp.logical_and(band == 0, i == f)

            @pl.when(self_)
            def _():
                local(src, dst, 1)

            @pl.when(jnp.logical_not(self_))
            def _():
                remote(src, dst, 1, (band, i))

            return carry

        lax.fori_loop(0, peers, send_old, 0)

    wait(got_ref, 1, 0)
    wait(old_ref, 1, 1)

    slot = got_ref[:, 8, :]
    want = (2 * lax.broadcasted_iota(jnp.int32, (peers, tile), 1) + q % 2).astype(jnp.float32)
    pick = jnp.where(slot == want, 1.0, 0.0)
    for r in range(8):
        add = lax.dot_general(pick, got_ref[:, r, :], (((0,), (0,)), ((), ())), precision=HI, preferred_element_type=jnp.float32)
        part_ref[:, r, :] = old_ref[:, r, :] + add[0:32]

    panel_mine = panel_ref.at[:, z, half, :, lanes(q)]
    diag_mine = diag_ref.at[:, z, half, :, lanes(q)]
    local(part_ref, panel_mine, 2)

    @pl.when(x == 0)
    def _():
        local(part_ref.at[0:4], diag_mine, 3)

        def send_x(k, carry):
            remote(part_ref.at[0:4], diag_mine, 3, (k, f))
            return carry

        lax.fori_loop(1, leafs, send_x, 0)

    wait(diag_mine, 1, 3)
    wait(panel_mine, 1, 2)

    def along_z(ref, stage):
        def go(k, carry):
            view = ref.at[:, z, half, :, lanes(q)]
            remote(view, view, stage, (x, device(lax.rem(z + k, NZ), y, c)))
            return carry

        lax.fori_loop(1, NZ, go, 0)

    def along_y(ref, stage):
        def go(k, carry):
            view = ref.at[:, :, half, :, lanes(q)]
            remote(view, view, stage, (x, device(z, lax.rem(y + k, NY), c)))
            return carry

        lax.fori_loop(1, NY, go, 0)

    def across(ref, stage):
        for h in range(2):
            view = ref.at[:, :, :, :, lanes(2 * h + c)]
            remote(view, view, stage, (x, device(z, y, 1 - c)))

    def views(ref, axis):
        if axis == 0:
            return ref.at[:, pl.ds(0, NZ - 1), half, :, lanes(q)]
        if axis == 1:
            return ref.at[:, :, 0, :, pl.ds(0, (NY - 1) * tile)]
        return ref.at[:, :, :, :, pl.ds(0, 2 * tile)]

    along_z(diag_ref, 4)
    along_z(panel_ref, 5)
    wait(views(diag_ref, 0), 1, 4)
    along_y(diag_ref, 6)
    wait(views(diag_ref, 1), 1, 6)
    across(diag_ref, 8)
    wait(views(panel_ref, 0), 1, 5)
    along_y(panel_ref, 7)
    wait(views(diag_ref, 2), 1, 8)
    wait(views(panel_ref, 1), 1, 7)
    across(panel_ref, 9)
    wait(views(panel_ref, 2), 1, 9)

    rows = panel_ref.at[pl.ds(2 * place, 2)]

    @pl.when(x == band)
    def _():
        local(rows, mine_ref, 10)

        def send_rows(k, carry):
            remote(rows, mine_ref, 10, (lax.rem(x + k, leafs), f))
            return carry

        lax.fori_loop(1, leafs, send_rows, 0)

    wait(mine_ref, 1, 10)

    wait(small_ref.at[pl.ds(0, peers - 1)], 0, 0)

    @pl.when(x == 0)
    def _():
        @pl.when(band == 0)
        def _():
            wait(turned_ref.at[:, pl.ds(0, 15), :, :], 0, 1)
            wait(turned_ref.at[:, 0, :, pl.ds(0, 3 * tile)], 0, 1)

        @pl.when(band != 0)
        def _():
            wait(turned_ref, 0, 1)

        wait(part_ref.at[pl.ds(0, 4 * (leafs - 1))], 0, 3)

    wait(views(diag_ref, 0), 0, 4)
    wait(views(panel_ref, 0), 0, 5)
    wait(views(diag_ref, 1), 0, 6)
    wait(views(panel_ref, 1), 0, 7)
    wait(views(diag_ref, 2), 0, 8)
    wait(views(panel_ref, 2), 0, 9)

    @pl.when(x == band)
    def _():
        wait(panel_ref.at[pl.ds(0, 2 * (leafs - 1))], 0, 10)


def panels(mesh_shape, small, turned):
    f32 = jnp.float32
    leafs, peers = mesh_shape["leaf"], mesh_shape["front"]
    vm = pl.BlockSpec(memory_space=pltpu.VMEM)
    panel, diag, mine, got = pl.pallas_call(
        functools.partial(panel_kernel, leafs),
        out_shape=(
            jax.ShapeDtypeStruct((32, NZ, 2, 8, 512), f32),
            jax.ShapeDtypeStruct((4, NZ, 2, 8, 512), f32),
            jax.ShapeDtypeStruct((2, NZ, 2, 8, 512), f32),
            jax.ShapeDtypeStruct((peers, 16, 128), f32),
        ),
        in_specs=[vm, vm],
        out_specs=(vm, vm, vm, vm),
        scratch_shapes=[
            pltpu.VMEM((32, 8, 128), f32),
            pltpu.VMEM((32, 8, 128), f32),
            pltpu.SemaphoreType.DMA((2, 11)),
        ],
        compiler_params=pltpu.CompilerParams(has_side_effects=True),
        name="panels",
    )(small, turned.reshape(2, 16, 8, 512))
    return panel.reshape(4096, 512), diag.reshape(512, 512), mine.reshape(256, 512), got


def dot(a, b, ca=1, cb=0):
    return lax.dot_general(a, b, (((ca,), (cb,)), ((), ())), precision=HI, preferred_element_type=jnp.float32)


def factor_inverse(a, m_ref, out_ref):
    n = 128
    row = lax.broadcasted_iota(jnp.int32, (n, n), 0)
    col = lax.broadcasted_iota(jnp.int32, (n, n), 1)
    m_ref[:, 0:n] = a
    m_ref[:, n : 2 * n] = jnp.where(row == col, 1.0, 0.0)
    sub = lax.broadcasted_iota(jnp.int32, (8, n), 0)
    lane = lax.broadcasted_iota(jnp.int32, (8, n), 1)

    def group(g, carry):
        start = pl.multiple_of(g * 8, 8)
        left = m_ref[pl.ds(start, 8), 0:n]
        right = m_ref[pl.ds(start, 8), n : 2 * n]
        cols = [jnp.broadcast_to(left[:, k : k + 1], (8, n)) for k in range(8)]
        scale = jnp.ones((8, n), jnp.float32)
        for j in range(8):
            pivot = jnp.broadcast_to(cols[j][j : j + 1, :], (8, n))
            below = jnp.where(sub > j, cols[j], 0.0) / pivot
            scale = jnp.where(sub == j, pivot, scale)
            for k in range(j + 1, 8):
                cols[k] = cols[k] - below * jnp.broadcast_to(cols[k][j : j + 1, :], (8, n))
            left = left - below * jnp.broadcast_to(left[j : j + 1, :], (8, n))
            right = right - below * jnp.broadcast_to(right[j : j + 1, :], (8, n))
        scale = lax.rsqrt(scale)
        left = left * scale
        right = right * scale
        out_ref[pl.ds(start, 8), :] = right
        turned = pltpu.roll(left, start, axis=1)
        turned = jnp.where(lane >= start + 8, turned, 0.0)
        m_ref[:, 0:n] = pltpu.roll(m_ref[:, 0:n] - dot(turned, left, 0, 0), n - 8, axis=1)
        m_ref[:, n : 2 * n] = m_ref[:, n : 2 * n] - dot(turned, right, 0, 0)
        return carry

    lax.fori_loop(0, n // 8, group, 0)


def factor_inverse_256(a, m_ref, p_ref, q_ref, out_ref):
    n = 128
    factor_inverse(a[:n, :n], m_ref, p_ref)
    p = p_ref[...]
    low = dot(a[n:, :n], p, 1, 1)
    factor_inverse(a[n:, n:] - dot(low, low, 1, 1), m_ref, q_ref)
    q = q_ref[...]
    out_ref[:n, :n] = p
    out_ref[:n, n:] = jnp.zeros((n, n), jnp.float32)
    out_ref[n:, n:] = q
    out_ref[n:, :n] = -dot(q, dot(low, p))


def weights_kernel(where_ref, d_ref, xc_ref, high_ref, low_ref, m_ref, p_ref, q_ref, c1_ref, c2_ref):
    w = 256
    column = where_ref[0]
    d11 = d_ref[0:w, 0:w]
    factor_inverse_256(0.5 * (d11 + d11.T), m_ref, p_ref, q_ref, c1_ref)
    c1 = c1_ref[...]
    low = dot(d_ref[w:, 0:w], c1, 1, 1)
    d22 = d_ref[w:, w:] - dot(low, low, 1, 1)
    factor_inverse_256(0.5 * (d22 + d22.T), m_ref, p_ref, q_ref, c2_ref)
    c2 = c2_ref[...]
    b = dot(c1, low, 0, 1)
    lc1 = dot(xc_ref[:, 0:w], c1, 1, 1)
    lc2 = dot(xc_ref[:, w:] - dot(lc1, low, 1, 1), c2, 1, 1)
    w1 = dot(c1, lc1, 0, 1)
    w2 = dot(c2, lc2, 0, 1)
    row = lax.broadcasted_iota(jnp.int32, (w, w), 0)
    col = lax.broadcasted_iota(jnp.int32, (w, w), 1)
    eye = jnp.where(row == col, 1.0, 0.0)
    first = column == 0
    second = column == 1
    c1t = dot(c1, eye, 0, 0)
    c2t = dot(c2, eye, 0, 0)
    w1 = jnp.where(first, -c1t, w1)
    w2 = jnp.where(second, -c2t, w2)
    none = jnp.zeros((w, w), jnp.float32)

    def put(kind, rows, value):
        high_ref[kind, rows, :], low_ref[kind, rows, :] = split(value)

    w2 = jnp.where(first, none, w2)
    top = jnp.where(first, w1, jnp.where(second, -dot(b, w2), w1 - dot(b, w2)))
    put(0, slice(0, w), jnp.where(first, w1, none))
    put(0, slice(w, 2 * w), none)
    put(1, slice(0, w), jnp.where(second, top, w1))
    put(1, slice(w, 2 * w), jnp.where(second, w2, none))
    put(2, slice(0, w), top)
    put(2, slice(w, 2 * w), w2)


def weights(column, d, xc):
    w = 256
    f32 = jnp.float32
    vm = pl.BlockSpec(memory_space=pltpu.VMEM)
    return pl.pallas_call(
        weights_kernel,
        out_shape=(jax.ShapeDtypeStruct((3, 2 * w, w), jnp.bfloat16),) * 2,
        in_specs=[pl.BlockSpec(memory_space=pltpu.SMEM), vm, vm],
        out_specs=(vm, vm),
        scratch_shapes=[
            pltpu.VMEM((128, 256), f32),
            pltpu.VMEM((128, 128), f32),
            pltpu.VMEM((128, 128), f32),
            pltpu.VMEM((w, w), f32),
            pltpu.VMEM((w, w), f32),
        ],
        name="weights",
    )(column, d, xc)


def shards(mesh_shape, front, updates, target_owner, target_slot):
    peers = mesh_shape["front"]
    big, small, turned = sort_blocks(target_owner, target_slot, updates, front, peers)
    arrived = lax.all_to_all(big, "front", split_axis=0, concat_axis=0, tiled=True)
    panel, diag, mine, got = panels(mesh_shape, small, turned)
    column = lax.axis_index("front").astype(jnp.int32)
    band = lax.axis_index("leaf").astype(jnp.int32)
    where = jnp.stack([column, band])
    labels = got[:, 9, 0].astype(jnp.int32)
    high, low = weights(where, diag, mine)
    return finish(where, labels, front, panel, arrived, high, low)


def solution(mesh):
    return jax.shard_map(
        functools.partial(shards, dict(mesh.shape)),
        mesh=mesh,
        in_specs=(
            P("leaf", "front"),
            P(("leaf", "front"), None, None),
            P(("leaf", "front")),
            P(("leaf", "front")),
        ),
        out_specs=P("leaf", "front"),
        check_vma=False,
    )
```

time: 939 us -> 317 us (0.34); the launches traced: 928 us -> 316 us
  waiting for transfers between devices: 659 us -> 0.01 us
  Pallas kernels: 0 us -> 301 us
  other arithmetic: 139 us -> 3.26 us
  matrix products: 45.1 us -> 0 us
  local copies, waits for them, and re-layouts: 44.6 us -> 0 us
  between operations: 16.7 us -> 0.03 us
  starting transfers between devices: 23 us -> 11.8 us
    psum x6 -> x0, waiting for transfers between devices: 577 us -> none  [spread(): return lax.psum(kept, axis)]
    pallas_call x0 -> x4, Pallas kernels: none -> 301 us  [the longest x1 230 us: panels(): pl.pallas_call(functools.partial(panel_kernel, leafs), out_shape=(jax.Sha...]
    another operation x18 -> x1, other arithmetic: 108 us -> 0.56 us  [shards(): where = jnp.stack([column, band])]
    all_to_all x2 -> x1, waiting for transfers between devices: 81.1 us -> 0.01 us  [shards(): lax.all_to_all(big, 'front', split_axis=0, concat_axis=0, tiled=True)]
    dot_general x4 -> x0, matrix products: 42.4 us -> none  [the longest x2 25.7 us: eliminate(): updated = shard - jnp.dot(trail, across.T, precision=lax.Precision.HIGHEST)]
    scatter-add x1 -> x0, other arithmetic: 13.8 us -> none  [assemble(): grid = grid.at[places // col_tiles, :, places % col_tiles, :].add(arrived)]
    select_n x6 -> x0, other arithmetic: 13.6 us -> none  [the longest x5 12.8 us: spread(): jnp.where(lax.axis_index(axis) == source, value, 0).astype(value.dtype)]
    reshape x2 -> x0, local copies, waits for them, and re-layouts: 10.5 us -> none  [assemble(): grid = front.reshape(nrows // tile, tile, col_tiles, tile)]
  transfers between devices with their start and end apart: 8 -> 1, of which waited for: 7 -> 0; matrix products, arithmetic and copies ran while one was open for 2% -> 1% of each run, Pallas kernels for 0% -> 88%
where the time goes in v1:
time: 317 us; the launch traced here: 316 us
  Pallas kernels  301 us (95%)
  starting transfers between devices  11.8 us (4%)
  other arithmetic  3.26 us (1%)
    pallas_call x1, Pallas kernels, panels(): pl.pallas_call(functools.partial(panel_kernel, leafs), out_shape=(jax.Sha...  230 us
    pallas_call x1, Pallas kernels, weights(): pl.pallas_call(weights_kernel, out_shape=(jax.ShapeDtypeStruct((3, 2 * w,...  50 us
    pallas_call x1, Pallas kernels, finish(): pl.pallas_call(finish_kernel, grid=(nrows // 256,), out_shape=jax.ShapeDt...  17.7 us
    all_to_all x1, starting transfers between devices, shards(): lax.all_to_all(big, 'front', split_axis=0, concat_axis=0, tiled=True)  11.8 us
  transfers between devices with their start and end apart: 1, of which 0 were waited for; matrix products, arithmetic and copies ran while one was open for 1% of the time, Pallas kernels for 88%

profile of v1, /device:TPU:65, one launch (start us, length us, event | category | flops | bytes accessed | tf_op | source)
XLA Modules:
  0.0 316.4 jit_solution(8916981658434868633)
XLA Ops:
  0.0 4.0 %sort_blocks.1 = (f32[64,128,128]{2,1,0:T(8,128)}, f32[64,16,128]{2,1,0:T(8,128)}, f32[256,512]{1,0:T(8,128)}) custom-call(s32[32]{0:T(128)} %owner_ref.1, s32[32]{0:T(128)} %slot_ref.1, f32[32,128,128]{2,1,0:T(8,128)} %updates_ref.1, f32[4096,256]{1,0:T(8,128)} %front_ref.1), custom_call_target="tpu_custom_call" | custom-call | tf_op jit(solution)/shard_map/sort_blocks/pallas_call | solution.py:57
  4.0 11.8 %all-to-all-start = ((f32[64,128,128]{2,1,0:T(8,128)}), f32[64,128,128]{2,1,0:T(8,128)}, u32[]{:S(2)}, u32[]{:S(2)}) async-start(f32[64,128,128]{2,1,0:T(8,128)} %get-tuple-element.18), calls=%async_computation | async-start | bytes 8388608 | tf_op jit(solution)/shard_map/all_to_all | solution.py:457
  15.8 229.7 %panels.1 = (f32[32,8,2,8,512]{4,3,2,1,0:T(8,128)}, f32[4,8,2,8,512]{4,3,2,1,0:T(8,128)}, f32[2,8,2,8,512]{4,3,2,1,0:T(8,128)}, f32[64,16,128]{2,1,0:T(8,128)}) custom-call(f32[64,16,128]{2,1,0:T(8,128)} %get-tuple-element.14.small_ref, f32[2,16,8,512]{3,2,1,0:T(8,128)} %bitcast.8), custom_call_target="tpu_custom_call" | custom-call | tf_op jit(solution)/shard_map/panels/pallas_call | solution.py:321
  245.5 0.6 pad_add_fusion.where_ref
  246.0 50.0 %weights.1 = (bf16[3,512,256]{2,1,0:T(8,128)(2,1)}, bf16[3,512,256]{2,1,0:T(8,128)(2,1)}) custom-call(s32[2]{0:T(128)} %pad_add_fusion.where_ref, f32[512,512]{1,0:T(8,128)} %bitcast.7, f32[256,512]{1,0:T(8,128)} %bitcast.9), custom_call_target="tpu_custom_call" | custom-call | tf_op jit(solution)/shard_map/weights/pallas_call | solution.py:438
  296.0 2.7 convert_reduce_fusion.label_ref
  298.7 0.0 all-to-all-done.arrived_ref
  298.7 17.7 %finish.1 = f32[4096,256]{1,0:T(8,128)} custom-call(s32[2]{0:T(128)} %pad_add_fusion.where_ref, s32[64]{0:T(128)} %convert_reduce_fusion.label_ref, f32[4096,256]{1,0:T(8,128)} %front_ref.1, f32[4096,512]{1,0:T(8,128)} %bitcast.6, f32[64,128,128]{2,1,0:T(8,128)} %all-to-all-done.arrived_ref, bf16[3,512,256]{2,1,0:T(8,128)(2,1)} %get-tuple-element.21.high_ref, ...), custom_call_target="tpu_custom_call" | custom-call | tf_op jit(solution)/shard_map/finish/pallas_call | solution.py:128
Async XLA Ops:
  4.0 294.8 %all-to-all-start = ((f32[64,128,128]{2,1,0:T(8,128)}), f32[64,128,128]{2,1,0:T(8,128)}, u32[]{:S(2)}, u32[]{:S(2)}) async-start(f32[64,128,128]{2,1,0:T(8,128)} %get-tuple-element.18), calls=%async_computation | async-start | bytes 8388608 | tf_op jit(solution)/shard_map/all_to_all | solution.py:457

commit v2 on v1

--- a/solution.py
+++ b/solution.py
@@ -89,16 +89,18 @@
     )
 
 
-def finish_kernel(where_ref, label_ref, front_ref, panel_ref, arrived_ref, high_ref, low_ref, out_ref, total_ref):
+def finish_kernel(label_ref, rest_ref, arrived_ref, out_ref, total_ref):
     step = pl.program_id(0)
     tile = 128
+    column = lax.axis_index("front")
+    band = lax.axis_index("leaf")
 
     @pl.when(step == 0)
     def _():
         total_ref[...] = jnp.zeros_like(total_ref)
 
         def add(j, carry):
-            slot = label_ref[j]
+            slot = label_ref[j, 0]
 
             @pl.when(slot >= 0)
             def _():
@@ -108,46 +110,41 @@
 
         lax.fori_loop(0, arrived_ref.shape[0], add, 0)
 
-    column, band = where_ref[0], where_ref[1]
-    kind = jnp.where(band == 0, jnp.minimum(step, 2), 2)
-    minus = product(panel_ref[...], (high_ref[kind], low_ref[kind]))
-    keep = jnp.logical_or(column >= 2, jnp.logical_and(column == 1, kind == 0))
-    for h in range(2):
+    top = jnp.logical_and(band == 0, step == 0)
+    for h in range(4):
         for k in range(2):
             rows = slice(h * tile, h * tile + tile)
             cols = slice(k * tile, k * tile + tile)
-            base = front_ref[rows, cols] + total_ref[step * 4 + h * 2 + k]
-            out_ref[rows, cols] = jnp.where(keep, base, 0.0) - minus[rows, cols]
-
-
-def finish(where, labels, front, panel, arrived, high, low):
-    nrows, width = front.shape
+            keep = jnp.logical_or(column >= 2, jnp.logical_and(column == 1, jnp.logical_and(top, h < 2)))
+            out_ref[rows, cols] = rest_ref[rows, cols] + jnp.where(keep, total_ref[step * 8 + h * 2 + k], 0.0)
+
+
+def finish(labels, rest, arrived):
+    nrows, width = rest.shape
     peers, tile = arrived.shape[:2]
-    smem = pl.BlockSpec(memory_space=pltpu.SMEM)
-    one = pl.Buffered(buffer_count=1)
     return pl.pallas_call(
         finish_kernel,
-        grid=(nrows // 256,),
+        grid=(nrows // 512,),
         out_shape=jax.ShapeDtypeStruct((nrows, width), jnp.float32),
         in_specs=[
-            smem,
-            smem,
-            pl.BlockSpec((256, width), lambda i: (i, 0)),
-            pl.BlockSpec((256, 2 * width), lambda i: (i, 0)),
-            pl.BlockSpec(arrived.shape, lambda i: (0, 0, 0), pipeline_mode=one),
-            pl.BlockSpec(high.shape, lambda i: (0, 0, 0), pipeline_mode=one),
-            pl.BlockSpec(low.shape, lambda i: (0, 0, 0), pipeline_mode=one),
+            pl.BlockSpec(memory_space=pltpu.SMEM),
+            pl.BlockSpec((512, width), lambda i: (i, 0)),
+            pl.BlockSpec(arrived.shape, lambda i: (0, 0, 0), pipeline_mode=pl.Buffered(buffer_count=1)),
         ],
-        out_specs=pl.BlockSpec((256, width), lambda i: (i, 0)),
+        out_specs=pl.BlockSpec((512, width), lambda i: (i, 0)),
         scratch_shapes=[pltpu.VMEM((64, tile, tile), jnp.float32)],
         name="finish",
-    )(where, labels, front, panel, arrived, high, low)
-
-
+    )(labels, rest, arrived)
+
+
+MESH = pl.DeviceIdType.MESH
 NZ, NY, NC = 8, 4, 2
 
 
-def panel_kernel(leafs, small_ref, turned_ref, panel_ref, diag_ref, mine_ref, got_ref, old_ref, part_ref, sems):
+def panel_kernel(
+    leafs, plan, big_ref, small_ref, turned_ref, front_ref, rest_ref, arrived_ref, label_ref,
+    panel_ref, diag_ref, mine_ref, got_ref, old_ref, part_ref, high_ref, low_ref, m_ref, p_ref, q_ref, c1_ref, c2_ref, sems,
+):
     peers = got_ref.shape[0]
     tile = 128
     x = lax.axis_index("leaf")
@@ -165,7 +162,7 @@
     def remote(src, dst, stage, target):
         pltpu.make_async_remote_copy(
             src_ref=src, dst_ref=dst, send_sem=sems.at[0, stage], recv_sem=sems.at[1, stage],
-            device_id=target, device_id_type=pl.DeviceIdType.MESH,
+            device_id=target, device_id_type=MESH,
         ).start()
 
     def local(src, dst, stage):
@@ -173,6 +170,29 @@
 
     def wait(ref, which, stage):
         pltpu.make_async_copy(ref, ref, sems.at[which, stage]).wait()
+
+    barrier = pltpu.get_barrier_semaphore()
+    total = leafs * peers
+    me = x * peers + f
+
+    def greet(k, carry):
+        d = lax.rem(me + k, total)
+        pl.semaphore_signal(barrier, inc=1, device_id=(d // peers, d % peers), device_id_type=MESH)
+        return carry
+
+    lax.fori_loop(1, total, greet, 0)
+    pl.semaphore_wait(barrier, total - 1)
+
+    def send_blocks(point):
+        first, last = plan.get(point, (0, 0))
+
+        def go(k, carry):
+            d = lax.rem(f + k, peers)
+            remote(big_ref.at[d], arrived_ref.at[f], 11, (x, d))
+            return carry
+
+        if last > first:
+            lax.fori_loop(first, last, go, 0)
 
     local(small_ref.at[f], got_ref.at[f], 0)
 
@@ -205,6 +225,9 @@
 
         lax.fori_loop(0, peers, send_old, 0)
 
+    send_blocks("start")
+    local(big_ref.at[f], arrived_ref.at[f], 11)
+    local(front_ref, rest_ref, 12)
     wait(got_ref, 1, 0)
     wait(old_ref, 1, 1)
 
@@ -212,12 +235,11 @@
     want = (2 * lax.broadcasted_iota(jnp.int32, (peers, tile), 1) + q % 2).astype(jnp.float32)
     pick = jnp.where(slot == want, 1.0, 0.0)
     for r in range(8):
-        add = lax.dot_general(pick, got_ref[:, r, :], (((0,), (0,)), ((), ())), precision=HI, preferred_element_type=jnp.float32)
+        add = dot(pick, got_ref[:, r, :], 0, 0)
         part_ref[:, r, :] = old_ref[:, r, :] + add[0:32]
 
     panel_mine = panel_ref.at[:, z, half, :, lanes(q)]
     diag_mine = diag_ref.at[:, z, half, :, lanes(q)]
-    local(part_ref, panel_mine, 2)
 
     @pl.when(x == 0)
     def _():
@@ -229,8 +251,9 @@
 
         lax.fori_loop(1, leafs, send_x, 0)
 
+    local(part_ref, panel_mine, 2)
+    label_ref[...] = got_ref[:, 9, :].astype(jnp.int32)
     wait(diag_mine, 1, 3)
-    wait(panel_mine, 1, 2)
 
     def along_z(ref, stage):
         def go(k, carry):
@@ -261,31 +284,63 @@
         return ref.at[:, :, :, :, pl.ds(0, 2 * tile)]
 
     along_z(diag_ref, 4)
+    wait(panel_mine, 1, 2)
     along_z(panel_ref, 5)
+    send_blocks("dz")
     wait(views(diag_ref, 0), 1, 4)
     along_y(diag_ref, 6)
+    send_blocks("dy")
     wait(views(diag_ref, 1), 1, 6)
     across(diag_ref, 8)
     wait(views(panel_ref, 0), 1, 5)
     along_y(panel_ref, 7)
+    send_blocks("py")
     wait(views(diag_ref, 2), 1, 8)
-    wait(views(panel_ref, 1), 1, 7)
-    across(panel_ref, 9)
-    wait(views(panel_ref, 2), 1, 9)
 
     rows = panel_ref.at[pl.ds(2 * place, 2)]
 
-    @pl.when(x == band)
-    def _():
-        local(rows, mine_ref, 10)
-
-        def send_rows(k, carry):
-            remote(rows, mine_ref, 10, (lax.rem(x + k, leafs), f))
-            return carry
-
-        lax.fori_loop(1, leafs, send_rows, 0)
-
-    wait(mine_ref, 1, 10)
+    def hook0():
+        send_blocks("h0")
+
+    def hook1():
+        send_blocks("h1")
+
+    def hook2():
+        send_blocks("h2")
+
+    def hook3():
+        wait(views(panel_ref, 1), 1, 7)
+        across(panel_ref, 9)
+        send_blocks("h3")
+        wait(views(panel_ref, 2), 1, 9)
+
+        @pl.when(x == band)
+        def _():
+            local(rows, mine_ref, 10)
+
+            def send_rows(k, carry):
+                remote(rows, mine_ref, 10, (lax.rem(x + k, leafs), f))
+                return carry
+
+            lax.fori_loop(1, leafs, send_rows, 0)
+
+        wait(mine_ref, 1, 10)
+
+    d2 = diag_ref.reshape(512, 512)
+    low = panel_inverses(d2, m_ref, p_ref, q_ref, c1_ref, c2_ref, (hook0, hook1, hook2, hook3))
+    panel_weights(f, low, c1_ref, c2_ref, mine_ref.reshape(256, 512), high_ref, low_ref)
+    wait(rest_ref, 1, 12)
+    x2 = panel_ref.reshape(4096, 512)
+
+    def subtract(step, carry):
+        kind = jnp.where(x == 0, jnp.minimum(step, 2), 2)
+        at = pl.ds(pl.multiple_of(step * 256, 256), 256)
+        minus = product(x2[at, :], (high_ref[kind], low_ref[kind]))
+        keep = jnp.logical_or(f >= 2, jnp.logical_and(f == 1, kind == 0))
+        rest_ref[at, :] = jnp.where(keep, rest_ref[at, :], 0.0) - minus
+        return carry
+
+    lax.fori_loop(0, 16, subtract, 0)
 
     wait(small_ref.at[pl.ds(0, peers - 1)], 0, 0)
 
@@ -313,30 +368,46 @@
     def _():
         wait(panel_ref.at[pl.ds(0, 2 * (leafs - 1))], 0, 10)
 
-
-def panels(mesh_shape, small, turned):
-    f32 = jnp.float32
+    wait(big_ref.at[pl.ds(0, peers - 1)], 0, 11)
+    wait(arrived_ref, 1, 11)
+
+
+PLAN = {"py": (1, 22), "h0": (22, 43), "h1": (43, 64)}
+
+
+def panels(mesh_shape, big, small, turned, front):
+    f32, bf16 = jnp.float32, jnp.bfloat16
     leafs, peers = mesh_shape["leaf"], mesh_shape["front"]
     vm = pl.BlockSpec(memory_space=pltpu.VMEM)
-    panel, diag, mine, got = pl.pallas_call(
-        functools.partial(panel_kernel, leafs),
+    hbm = pl.BlockSpec(memory_space=pl.ANY)
+    return pl.pallas_call(
+        functools.partial(panel_kernel, leafs, PLAN),
         out_shape=(
-            jax.ShapeDtypeStruct((32, NZ, 2, 8, 512), f32),
-            jax.ShapeDtypeStruct((4, NZ, 2, 8, 512), f32),
-            jax.ShapeDtypeStruct((2, NZ, 2, 8, 512), f32),
-            jax.ShapeDtypeStruct((peers, 16, 128), f32),
+            jax.ShapeDtypeStruct(front.shape, f32),
+            jax.ShapeDtypeStruct(big.shape, f32),
+            jax.ShapeDtypeStruct((peers, 128), jnp.int32),
         ),
-        in_specs=[vm, vm],
-        out_specs=(vm, vm, vm, vm),
+        in_specs=[hbm, vm, vm, hbm],
+        out_specs=(vm, hbm, vm),
         scratch_shapes=[
+            pltpu.VMEM((32, NZ, 2, 8, 512), f32),
+            pltpu.VMEM((4, NZ, 2, 8, 512), f32),
+            pltpu.VMEM((2, NZ, 2, 8, 512), f32),
+            pltpu.VMEM((peers, 16, 128), f32),
             pltpu.VMEM((32, 8, 128), f32),
             pltpu.VMEM((32, 8, 128), f32),
-            pltpu.SemaphoreType.DMA((2, 11)),
+            pltpu.VMEM((3, 512, 256), bf16),
+            pltpu.VMEM((3, 512, 256), bf16),
+            pltpu.VMEM((128, 256), f32),
+            pltpu.VMEM((128, 128), f32),
+            pltpu.VMEM((128, 128), f32),
+            pltpu.VMEM((256, 256), f32),
+            pltpu.VMEM((256, 256), f32),
+            pltpu.SemaphoreType.DMA((2, 13)),
         ],
-        compiler_params=pltpu.CompilerParams(has_side_effects=True),
+        compiler_params=pltpu.CompilerParams(has_side_effects=True, collective_id=0),
         name="panels",
-    )(small, turned.reshape(2, 16, 8, 512))
-    return panel.reshape(4096, 512), diag.reshape(512, 512), mine.reshape(256, 512), got
+    )(big, small, turned.reshape(2, 16, 8, 512), front)
 
 
 def dot(a, b, ca=1, cb=0):
@@ -379,9 +450,10 @@
     lax.fori_loop(0, n // 8, group, 0)
 
 
-def factor_inverse_256(a, m_ref, p_ref, q_ref, out_ref):
+def factor_inverse_256(a, m_ref, p_ref, q_ref, out_ref, between):
     n = 128
     factor_inverse(a[:n, :n], m_ref, p_ref)
+    between()
     p = p_ref[...]
     low = dot(a[n:, :n], p, 1, 1)
     factor_inverse(a[n:, n:] - dot(low, low, 1, 1), m_ref, q_ref)
@@ -392,15 +464,21 @@
     out_ref[n:, :n] = -dot(q, dot(low, p))
 
 
-def weights_kernel(where_ref, d_ref, xc_ref, high_ref, low_ref, m_ref, p_ref, q_ref, c1_ref, c2_ref):
+def panel_inverses(d_ref, m_ref, p_ref, q_ref, c1_ref, c2_ref, hooks):
     w = 256
-    column = where_ref[0]
     d11 = d_ref[0:w, 0:w]
-    factor_inverse_256(0.5 * (d11 + d11.T), m_ref, p_ref, q_ref, c1_ref)
+    factor_inverse_256(0.5 * (d11 + d11.T), m_ref, p_ref, q_ref, c1_ref, hooks[0])
+    hooks[1]()
+    low = dot(d_ref[w:, 0:w], c1_ref[...], 1, 1)
+    d22 = d_ref[w:, w:] - dot(low, low, 1, 1)
+    factor_inverse_256(0.5 * (d22 + d22.T), m_ref, p_ref, q_ref, c2_ref, hooks[2])
+    hooks[3]()
+    return low
+
+
+def panel_weights(column, low, c1_ref, c2_ref, xc_ref, high_ref, low_ref):
+    w = 256
     c1 = c1_ref[...]
-    low = dot(d_ref[w:, 0:w], c1, 1, 1)
-    d22 = d_ref[w:, w:] - dot(low, low, 1, 1)
-    factor_inverse_256(0.5 * (d22 + d22.T), m_ref, p_ref, q_ref, c2_ref)
     c2 = c2_ref[...]
     b = dot(c1, low, 0, 1)
     lc1 = dot(xc_ref[:, 0:w], c1, 1, 1)
@@ -431,37 +509,11 @@
     put(2, slice(w, 2 * w), w2)
 
 
-def weights(column, d, xc):
-    w = 256
-    f32 = jnp.float32
-    vm = pl.BlockSpec(memory_space=pltpu.VMEM)
-    return pl.pallas_call(
-        weights_kernel,
-        out_shape=(jax.ShapeDtypeStruct((3, 2 * w, w), jnp.bfloat16),) * 2,
-        in_specs=[pl.BlockSpec(memory_space=pltpu.SMEM), vm, vm],
-        out_specs=(vm, vm),
-        scratch_shapes=[
-            pltpu.VMEM((128, 256), f32),
-            pltpu.VMEM((128, 128), f32),
-            pltpu.VMEM((128, 128), f32),
-            pltpu.VMEM((w, w), f32),
-            pltpu.VMEM((w, w), f32),
-        ],
-        name="weights",
-    )(column, d, xc)
-
-
 def shards(mesh_shape, front, updates, target_owner, target_slot):
     peers = mesh_shape["front"]
     big, small, turned = sort_blocks(target_owner, target_slot, updates, front, peers)
-    arrived = lax.all_to_all(big, "front", split_axis=0, concat_axis=0, tiled=True)
-    panel, diag, mine, got = panels(mesh_shape, small, turned)
-    column = lax.axis_index("front").astype(jnp.int32)
-    band = lax.axis_index("leaf").astype(jnp.int32)
-    where = jnp.stack([column, band])
-    labels = got[:, 9, 0].astype(jnp.int32)
-    high, low = weights(where, diag, mine)
-    return finish(where, labels, front, panel, arrived, high, low)
+    rest, arrived, labels = panels(mesh_shape, big, small, turned, front)
+    return finish(labels, rest, arrived)
 
 
 def solution(mesh):

time: 317 us -> 215 us (0.68)
  Pallas kernels: 301 us -> 213 us
  starting transfers between devices: 11.8 us -> 0 us
  other arithmetic: 3.26 us -> 0 us
    pallas_call x3 -> x2, Pallas kernels: 297 us -> 209 us  [the longest x1 200 us: panels(): pl.pallas_call(functools.partial(panel_kernel, leafs, PLAN), out_shape=(j...]
    all_to_all x1 -> x0, starting transfers between devices: 11.8 us -> none  [shards(): lax.all_to_all(big, 'front', split_axis=0, concat_axis=0, tiled=True)]
  transfers between devices with their start and end apart: 1 -> 0, of which waited for: 0 -> 0; matrix products, arithmetic and copies ran while one was open for 1% -> 0% of each run, Pallas kernels for 88% -> 0%
where the time goes in v2:
time: 215 us; the launch traced here: 213 us
  Pallas kernels  213 us (99%)
    pallas_call x1, Pallas kernels, panels(): pl.pallas_call(functools.partial(panel_kernel, leafs, PLAN), out_shape=(j...  200 us
    pallas_call x1, Pallas kernels, finish(): pl.pallas_call(finish_kernel, grid=(nrows // 512,), out_shape=jax.ShapeDt...  9.41 us

profile of v2, /device:TPU:65, one launch (start us, length us, event | category | flops | bytes accessed | tf_op | source)
XLA Modules:
  0.0 213.2 jit_solution(16669957625665153799)
XLA Ops:
  0.0 4.0 %sort_blocks.1 = (f32[64,128,128]{2,1,0:T(8,128)}, f32[64,16,128]{2,1,0:T(8,128)}, f32[256,512]{1,0:T(8,128)}) custom-call(s32[32]{0:T(128)} %owner_ref.1, s32[32]{0:T(128)} %slot_ref.1, f32[32,128,128]{2,1,0:T(8,128)} %updates_ref.1, f32[4096,256]{1,0:T(8,128)} %front_ref.1), custom_call_target="tpu_custom_call" | custom-call | tf_op jit(solution)/shard_map/sort_blocks/pallas_call | solution.py:57
  4.0 199.7 %panels.1 = (f32[4096,256]{1,0:T(8,128)}, f32[64,128,128]{2,1,0:T(8,128)}, s32[64,128]{1,0:T(8,128)}) custom-call(f32[64,128,128]{2,1,0:T(8,128)} %get-tuple-element.11.big_ref, f32[64,16,128]{2,1,0:T(8,128)} %get-tuple-element.12.small_ref, f32[2,16,8,512]{3,2,1,0:T(8,128)} %bitcast.1, f32[4096,256]{1,0:T(8,128)} %front_ref.1), custom_call_target="tpu_custom_call" | custom-call | tf_op jit(solution)/shard_map/panels/pallas_call | solution.py:383
  203.8 9.4 %finish.1 = f32[4096,256]{1,0:T(8,128)} custom-call(s32[64,128]{1,0:T(8,128)} %get-tuple-element.14.label_ref, f32[4096,256]{1,0:T(8,128)} %get-tuple-element.15.rest_ref, f32[64,128,128]{2,1,0:T(8,128)} %get-tuple-element.16.arrived_ref), custom_call_target="tpu_custom_call" | custom-call | tf_op jit(solution)/shard_map/finish/pallas_call | solution.py:125
